TPU v7x, 32 devices: a whole 2x2x4 slice. The times are simulated.
32 devices in a mesh: grp: 2 (over x), inp: 4 (over y, core), out: 4 (over z).
Axes of the slice: x: 2, y: 2, z: 4, core: 2. Of those that a mesh axis runs over, the one named last changes fastest.
Arguments:
- activations: bfloat16 [4, 512, 8192], P('grp', 'out', 'inp'), parts along dimension 0, may hold values from -6 to 6
- out_grads: bfloat16 [4, 512, 28672], P('grp', 'inp', 'out'), parts along dimension 0, may hold values from -6 to 6
- query_grads: bfloat16 [2, 28672, 8192], P(None, 'out', 'inp'), may hold values from -0.00036621094 to 0.00036621094
- token_ids: int32 [4, 512], P('grp'), parts along dimension 0, may hold values from 0 to 128255
- loss_mask: int32 [4, 512], P('grp'), parts along dimension 0, may hold values 0 or 1
Outputs:
- scores: float32 [2, 4, 512], P(None, 'grp'), parts along dimension 1
There are 2 independent parts, one for each index of `grp`. A program takes and returns all parts, laid end to end along the dimension named above; an argument that names none is the same for every part. Nothing has to cross between parts.
All inputs are finite; a program needn't handle non-finite values.
Results may differ from a plain program's by a relative error of at most 0.0003.
Values may be sent and summed in bfloat16 or wider, within the bound.
A program may use at most 128 MiB of HBM per device.

v0:
```python
import jax
import jax.numpy as jnp
from jax import lax
from jax.sharding import PartitionSpec as P


def shards(activations, out_grads, query_grads, token_ids, loss_mask):
    blocks = activations.shape[0]
    partials = []
    for number in range(blocks):
        gathered = lax.all_gather(activations[number], "out", axis=0, tiled=True)
        projected = jnp.einsum(
            "to,qoi->tqi",
            lax.all_gather(out_grads[number], "inp", axis=0, tiled=True),
            query_grads,
            preferred_element_type=jnp.float32,
        )
        partial_value = jnp.sum(projected * gathered.astype(jnp.float32)[:, None, :], axis=2)
        partial_value = lax.psum(partial_value, ("inp", "out"))
        partials.append(partial_value)
    stacked = jnp.stack(partials)
    equal = token_ids[:, :, None] == token_ids[:, None, :]
    counts = jnp.sum(equal.astype(jnp.int32), axis=2)
    weight = loss_mask.astype(jnp.float32) / counts.astype(jnp.float32)
    return jnp.transpose(stacked * weight[:, :, None], (2, 0, 1))


def solution(mesh):
    in_specs = (
        P("grp", "out", "inp"),
        P("grp", "inp", "out"),
        P(None, "out", "inp"),
        P("grp", None),
        P("grp", None),
    )
    out_specs = P(None, "grp", None)
    return jax.shard_map(shards, mesh=mesh, in_specs=in_specs, out_specs=out_specs, check_vma=False)
```

profile of v0, /device:TPU:0, one launch (start us, length us, event | category | flops | bytes accessed | tf_op | source)
XLA Modules:
  0.0 289.7 jit_solution(5545557528172188764)
XLA Ops:
  6.5 0.0 copy-start
  6.5 0.0 copy-start.1
  6.5 0.0 all-gather.15.cloned.1.call-start
  6.5 2.3 fusion.10
  8.9 0.0 all-gather.15.cloned.1.call-update
  8.9 0.0 all-gather.11.cloned.1.call-start
  8.9 0.7 all-gather.11.cloned.1.call-update
  9.6 0.0 all-gather.13.cloned.1.call-start
  9.7 4.1 %fusion.9 = (bf16[1,128,7168]{2,1,0:T(8,128)(2,1)}, bf16[1,128,7168]{2,1,0:T(8,128)(2,1)}) fusion(bf16[2,128,7168]{2,1,0:T(8,128)(2,1)} %param.6), kind=kLoop, calls=%fused_computation.12 | loop fusion | bytes 7340032 | tf_op jit(solution)/shard_map/slice | solution.py:14
  13.8 0.0 all-gather.13.cloned.1.call-update
  13.8 0.0 all-gather.9.cloned.1.call-start
  13.9 0.5 all-gather.9.cloned.1.call-update
  14.4 0.0 copy-done
  14.4 0.4 convert_reduce_fusion
  14.8 0.0 copy-done.1
  14.8 42.6 %all-gather.15.cloned.1.call-done = bf16[1,512,2048]{2,1,0:T(8,128)(2,1)} async-done(((bf16[1,128,2048]{2,1,0:T(8,128)(2,1)}), bf16[1,512,2048]{2,1,0:T(8,128)(2,1)}) %all-gather.15.cloned.1.call-update) | async-done | bytes 2097168 | tf_op jit(solution)/shard_map/all_gather | solution.py:11
  57.4 4.1 %bitcast_convert_fusion = f32[512,2048]{1,0:T(8,128)} fusion(bf16[1,512,2048]{2,1,0:T(8,128)(2,1)} %all-gather.15.cloned.1.call-done), kind=kLoop, calls=%fused_computation.6 | loop fusion | flops 1048576 | bytes 6291456 | tf_op jit(solution)/shard_map/convert_element_type | solution.py:18
  61.5 42.0 %all-gather.11.cloned.1.call-done = bf16[1,512,2048]{2,1,0:T(8,128)(2,1)} async-done(((bf16[1,128,2048]{2,1,0:T(8,128)(2,1)}), bf16[1,512,2048]{2,1,0:T(8,128)(2,1)}) %all-gather.11.cloned.1.call-update) | async-done | bytes 2097168 | tf_op jit(solution)/shard_map/all_gather | solution.py:11
  103.5 4.1 %bitcast_convert_fusion.1 = f32[512,2048]{1,0:T(8,128)} fusion(bf16[1,512,2048]{2,1,0:T(8,128)(2,1)} %all-gather.11.cloned.1.call-done), kind=kLoop, calls=%fused_computation.7 | loop fusion | flops 1048576 | bytes 6291456 | tf_op jit(solution)/shard_map/convert_element_type | solution.py:18
  107.6 48.6 %all-gather.13.cloned.1.call-done = bf16[1,512,7168]{2,1,0:T(8,128)(2,1)} async-done(((bf16[1,128,7168]{2,1,0:T(8,128)(2,1)}), bf16[1,512,7168]{2,1,0:T(8,128)(2,1)}) %all-gather.13.cloned.1.call-update) | async-done | bytes 7340048 | tf_op jit(solution)/shard_map/all_gather | solution.py:14
  156.2 39.0 %multiply_reduce_fusion = f32[512,2]{0,1:T(2,128)S(1)} fusion(f32[512,2048]{1,0:T(8,128)} %bitcast_convert_fusion, bf16[2,7168,2048]{2,1,0:T(8,128)(2,1)} %param.7, bf16[1,512,7168]{2,1,0:T(8,128)(2,1)} %all-gather.13.cloned.1.call-done), kind=kOutput, calls=%fused_computation | convolution fusion | flops 30068965376 | bytes 70258688 | tf_op jit(solution)/shard_map/to,qoi->tqi/dot_general | solution.py:12
  195.2 14.8 %all-gather.9.cloned.1.call-done = bf16[1,512,7168]{2,1,0:T(8,128)(2,1)} async-done(((bf16[1,128,7168]{2,1,0:T(8,128)(2,1)}), bf16[1,512,7168]{2,1,0:T(8,128)(2,1)}) %all-gather.9.cloned.1.call-update) | async-done | bytes 7340048 | tf_op jit(solution)/shard_map/all_gather | solution.py:14
  210.0 38.8 %multiply_reduce_fusion.1 = f32[512,2]{0,1:T(2,128)S(1)} fusion(f32[512,2048]{1,0:T(8,128)} %bitcast_convert_fusion.1, bf16[2,7168,2048]{2,1,0:T(8,128)(2,1)} %param.7, bf16[1,512,7168]{2,1,0:T(8,128)(2,1)} %all-gather.9.cloned.1.call-done), kind=kOutput, calls=%fused_computation.1 | convolution fusion | flops 30068965376 | bytes 70258688 | tf_op jit(solution)/shard_map/to,qoi->tqi/dot_general | solution.py:12
  248.8 33.8 %all-reduce = (f32[1,512,2]{1,0,2:T(1,128)S(1)}, f32[1,512,2]{1,0,2:T(1,128)S(1)}) all-reduce(f32[1,512,2]{1,0,2:T(1,128)S(1)} %stack.10, f32[1,512,2]{1,0,2:T(1,128)S(1)} %stack.9), channel_id=1, replica_groups=mesh['grp'=2,'inp'=4,'out'=4] {'inp','out'}, use_global_device_ids=true, to_apply=%region_3.0 | all-reduce | flops 2048 | bytes 16384 | tf_op jit(solution)/shard_map/psum | solution.py:19
  282.6 0.6 fusion.8
  (3 shorter events, 0.0 us)
Async XLA Ops:
  6.5 7.9 %copy-start = (s32[2,512]{1,0:T(2,128)S(1)}, s32[2,512]{1,0:T(2,128)}, u32[]{:S(2)}) copy-start(s32[2,512]{1,0:T(2,128)} %param.8) | copy-start | bytes 12292
  6.5 8.3 %copy-start.1 = (s32[2,512]{1,0:T(2,128)S(1)}, s32[2,512]{1,0:T(2,128)}, u32[]{:S(2)}) copy-start(s32[2,512]{1,0:T(2,128)} %param.9) | copy-start | bytes 12292
  6.5 50.9 %all-gather.15.cloned.1.call-start = ((), (), s32[]{:S(2)}) async-start(), calls=%async_computation.3 | async-start | bytes 2621440 | tf_op jit(solution)/shard_map/all_gather | solution.py:11
  8.9 94.6 %all-gather.11.cloned.1.call-start = ((), (), s32[]{:S(2)}) async-start(), calls=%async_computation.1 | async-start | bytes 2621440 | tf_op jit(solution)/shard_map/all_gather | solution.py:11
  9.6 146.6 %all-gather.13.cloned.1.call-start = ((), (), s32[]{:S(2)}) async-start(), calls=%async_computation.2 | async-start | bytes 9175040 | tf_op jit(solution)/shard_map/all_gather | solution.py:14
  13.8 196.1 %all-gather.9.cloned.1.call-start = ((), (), s32[]{:S(2)}) async-start(), calls=%async_computation | async-start | bytes 9175040 | tf_op jit(solution)/shard_map/all_gather | solution.py:14
Sparse Core Ops, SparseCore 0:
  9.0 48.3 all-gather.14
  59.0 44.4 all-gather.10
  105.0 51.1 all-gather.12
  157.6 52.2 all-gather.8
where the time goes:
time: 290 us
  waiting for transfers between devices  149 us (51%)
  matrix products  77.8 us (27%)
  blocking collectives  33.8 us (12%)
  between operations  13.2 us (5%)
  other arithmetic  9.25 us (3%)
  local copies, waits for them, and re-layouts  6.45 us (2%)
    all_gather x2, waiting for transfers between devices, shards(): gathered = lax.all_gather(activations[number], 'out', axis=0, tiled=True)  84.5 us
    dot_general x2, matrix products, shards(): jnp.einsum('to,qoi->tqi', lax.all_gather(out_grads[number], 'inp', axis=0...  77.8 us
    all_gather x2, waiting for transfers between devices, shards(): lax.all_gather(out_grads[number], 'inp', axis=0, tiled=True)  63.4 us
    psum x1, blocking collectives, shards(): partial_value = lax.psum(partial_value, ('inp', 'out'))  33.8 us
    convert_element_type x2, other arithmetic, shards(): gathered.astype(jnp.float32)[:, None, :]  8.22 us
  transfers between devices with their start and end apart: 4, of which 4 were waited for; matrix products, arithmetic and copies ran while one was open for 18% of the time, Pallas kernels for 0%

commit v1 on v0

--- a/solution.py
+++ b/solution.py
@@ -8,7 +8,23 @@
     blocks = activations.shape[0]
     partials = []
     for number in range(blocks):
-        gathered = lax.all_gather(activations[number], "out", axis=0, tiled=True)
+        peers, index, rows = (
+            lax.axis_size("out"),
+            lax.axis_index("out"),
+            activations[number].shape[0],
+        )
+        right = [(i, (i + 1) % peers) for i in range(peers)]
+        out = jnp.zeros(
+            (*activations[number].shape[:0], peers * rows, *activations[number].shape[0 + 1 :]),
+            activations[number].dtype,
+        )
+        block = activations[number]
+        for lap in range(peers):
+            source = (index - lap) % peers
+            out = lax.dynamic_update_slice_in_dim(out, block, source * rows, axis=0)
+            if lap < peers - 1:
+                block = lax.ppermute(block, "out", right)
+        gathered = out
         projected = jnp.einsum(
             "to,qoi->tqi",
             lax.all_gather(out_grads[number], "inp", axis=0, tiled=True),

time: 290 us -> 206 us (0.71)
  waiting for transfers between devices: 149 us -> 58 us
  local copies, waits for them, and re-layouts: 6.45 us -> 12 us
  starting transfers between devices: 0.12 us -> 4.68 us
    all_gather x2 -> x0, waiting for transfers between devices: 84.5 us -> none  [shards(): gathered = lax.all_gather(activations[number], 'out', axis=0, tiled=True)]
    all_gather x2, waiting for transfers between devices: 63.4 us -> 0.02 us  [shards(): lax.all_gather(out_grads[number], 'inp', axis=0, tiled=True)]
    ppermute x0 -> x6, waiting for transfers between devices: none -> 57.3 us  [shards(): block = lax.ppermute(block, 'out', right)]
    dynamic_update_slice x0 -> x8, local copies, waits for them, and re-layouts: none -> 4.85 us  [shards(): out = lax.dynamic_update_slice_in_dim(out, block, source * rows, axis=0)]
    ppermute x0 -> x6, starting transfers between devices: none -> 4.64 us  [shards(): block = lax.ppermute(block, 'out', right)]
  transfers between devices with their start and end apart: 4 -> 8, of which waited for: 4 -> 6; matrix products, arithmetic and copies ran while one was open for 18% -> 26% of each run, Pallas kernels for 0% -> 0%
where the time goes in v1:
time: 206 us
  matrix products  77.8 us (38%)
  waiting for transfers between devices  58 us (28%)
  blocking collectives  31.8 us (15%)
  between operations  13.6 us (7%)
  local copies, waits for them, and re-layouts  12 us (6%)
  other arithmetic  8.18 us (4%)
  starting transfers between devices  4.68 us (2%)
    dot_general x2, matrix products, shards(): jnp.einsum('to,qoi->tqi', lax.all_gather(out_grads[number], 'inp', axis=0...  77.8 us
    ppermute x6, waiting for transfers between devices, shards(): block = lax.ppermute(block, 'out', right)  57.3 us
    psum x1, blocking collectives, shards(): partial_value = lax.psum(partial_value, ('inp', 'out'))  31.8 us
    convert_element_type x2, other arithmetic, shards(): gathered.astype(jnp.float32)[:, None, :]  7.15 us
    dynamic_update_slice x8, local copies, waits for them, and re-layouts, shards(): out = lax.dynamic_update_slice_in_dim(out, block, source * rows, axis=0)  4.85 us
    ppermute x6, starting transfers between devices, shards(): block = lax.ppermute(block, 'out', right)  4.64 us
  transfers between devices with their start and end apart: 8, of which 6 were waited for; matrix products, arithmetic and copies ran while one was open for 26% of the time, Pallas kernels for 0%

profile of v1, /device:TPU:0, one launch (start us, length us, event | category | flops | bytes accessed | tf_op | source)
XLA Modules:
  0.0 206.1 jit_solution(16304264300216692948)
XLA Ops:
  6.5 0.0 all-gather.5.cloned.1.call-start
  6.5 4.1 %fusion.5 = (bf16[1,128,7168]{2,1,0:T(8,128)(2,1)}, bf16[1,128,7168]{2,1,0:T(8,128)(2,1)}) fusion(bf16[2,128,7168]{2,1,0:T(8,128)(2,1)} %param.6), kind=kLoop, calls=%fused_computation.20 | loop fusion | bytes 7340032 | tf_op jit(solution)/shard_map/slice | solution.py:30
  10.6 0.0 copy-start.1
  10.6 0.0 all-gather.5.cloned.1.call-update
  10.7 0.0 all-gather.7.cloned.1.call-start
  10.7 0.7 all-gather.7.cloned.1.call-update
  11.4 0.4 copy-done.1
  11.9 1.1 slice_bitcast_fusion.1
  13.0 3.1 %collective-permute-start = (bf16[128,2048]{1,0:T(8,128)(2,1)}, bf16[128,2048]{1,0:T(8,128)(2,1)}, u32[]{:S(2)}, u32[]{:S(2)}) collective-permute-start(bf16[128,2048]{1,0:T(8,128)(2,1)} %get-tuple-element.9), channel_id=1, source_target_pairs={{0,1},{1,2},{2,3},{3,0},{4,5},{5,6},{6,7},{7,4},{8,9},{9,10},{10,1... | collective-permute-start | bytes 1572872 | tf_op jit(solution)/shard_map/ppermute | solution.py:26
  16.0 1.6 collective-permute-start.3
  17.6 0.2 broadcast.12.clone.1
  17.8 0.0 copy-start.2
  17.9 0.0 copy-start.3
  17.9 0.0 copy-start
  17.9 0.2 broadcast.12.clone
  18.2 0.1 constant_dynamic-update-slice_fusion.3
  18.2 1.0 copy-done
  19.2 11.9 %collective-permute-done = bf16[128,2048]{1,0:T(8,128)(2,1)} collective-permute-done((bf16[128,2048]{1,0:T(8,128)(2,1)}, bf16[128,2048]{1,0:T(8,128)(2,1)}, u32[]{:S(2)}, u32[]{:S(2)}) %collective-permute-start) | collective-permute-done | bytes 524320 | tf_op jit(solution)/shard_map/ppermute | solution.py:26
  31.1 0.0 collective-permute-start.1
  31.1 0.0 copy-done.2
  31.1 0.4 convert_reduce_fusion
  31.5 10.8 %collective-permute-done.3 = bf16[128,2048]{1,0:T(8,128)(2,1)} collective-permute-done((bf16[128,2048]{1,0:T(8,128)(2,1)}, bf16[128,2048]{1,0:T(8,128)(2,1)}, u32[]{:S(2)}, u32[]{:S(2)}) %collective-permute-start.3) | collective-permute-done | bytes 524320 | tf_op jit(solution)/shard_map/ppermute | solution.py:26
  42.4 0.0 collective-permute-start.4
  42.4 0.0 copy-done.3
  42.4 1.9 constant_dynamic-update-slice_fusion.6
  44.3 9.1 %collective-permute-done.1 = bf16[128,2048]{1,0:T(8,128)(2,1)S(1)} collective-permute-done((bf16[128,2048]{1,0:T(8,128)(2,1)}, bf16[128,2048]{1,0:T(8,128)(2,1)S(1)}, u32[]{:S(2)}, u32[]{:S(2)}) %collective-permute-start.1) | collective-permute-done | bytes 524320 | tf_op jit(solution)/shard_map/ppermute | solution.py:26
  53.5 0.0 collective-permute-start.2
  53.5 1.1 constant_dynamic-update-slice_fusion.2
  54.6 10.1 %collective-permute-done.4 = bf16[128,2048]{1,0:T(8,128)(2,1)S(1)} collective-permute-done((bf16[128,2048]{1,0:T(8,128)(2,1)}, bf16[128,2048]{1,0:T(8,128)(2,1)S(1)}, u32[]{:S(2)}, u32[]{:S(2)}) %collective-permute-start.4) | collective-permute-done | bytes 524320 | tf_op jit(solution)/shard_map/ppermute | solution.py:26
  64.7 0.0 collective-permute-start.5
  64.7 0.8 constant_dynamic-update-slice_fusion.5
  65.6 10.3 %collective-permute-done.2 = bf16[128,2048]{1,0:T(8,128)(2,1)S(1)} collective-permute-done((bf16[128,2048]{1,0:T(8,128)(2,1)S(1)}, bf16[128,2048]{1,0:T(8,128)(2,1)S(1)}, u32[]{:S(2)}, u32[]{:S(2)}) %collective-permute-start.2) | collective-permute-done | bytes 524320 | tf_op jit(solution)/shard_map/ppermute | solution.py:26
  76.0 0.8 constant_dynamic-update-slice_fusion.4
  76.8 4.6 %convert_element_type.15 = f32[512,2048]{1,0:T(8,128)} convert(bf16[512,2048]{1,0:T(8,128)(2,1)} %constant_dynamic-update-slice_fusion.4) | non-fusion elementwise | flops 1048576 | bytes 6291456 | tf_op jit(solution)/shard_map/convert_element_type | solution.py:34
  81.4 4.9 %collective-permute-done.5 = bf16[128,2048]{1,0:T(8,128)(2,1)S(1)} collective-permute-done((bf16[128,2048]{1,0:T(8,128)(2,1)S(1)}, bf16[128,2048]{1,0:T(8,128)(2,1)S(1)}, u32[]{:S(2)}, u32[]{:S(2)}) %collective-permute-start.5) | collective-permute-done | bytes 524320 | tf_op jit(solution)/shard_map/ppermute | solution.py:26
  86.3 0.1 constant_dynamic-update-slice_fusion
  86.4 2.5 %convert_element_type.16 = f32[512,2048]{1,0:T(8,128)} convert(bf16[512,2048]{1,0:T(8,128)(2,1)S(1)} %constant_dynamic-update-slice_fusion) | non-fusion elementwise | flops 1048576 | bytes 6291456 | tf_op jit(solution)/shard_map/convert_element_type | solution.py:34
  88.9 0.0 all-gather.5.cloned.1.call-done
  88.9 39.0 %multiply_reduce_fusion.1 = f32[512,2]{0,1:T(2,128)S(1)} fusion(f32[512,2048]{1,0:T(8,128)} %convert_element_type.15, bf16[2,7168,2048]{2,1,0:T(8,128)(2,1)} %param.7, bf16[1,512,7168]{2,1,0:T(8,128)(2,1)} %all-gather.5.cloned.1.call-done), kind=kOutput, calls=%fused_computation.1 | convolution fusion | flops 30068965376 | bytes 70258688 | tf_op jit(solution)/shard_map/to,qoi->tqi/dot_general | solution.py:28
  127.9 0.0 all-gather.7.cloned.1.call-done
  128.0 38.8 %multiply_reduce_fusion = f32[512,2]{0,1:T(2,128)S(1)} fusion(f32[512,2048]{1,0:T(8,128)} %convert_element_type.16, bf16[2,7168,2048]{2,1,0:T(8,128)(2,1)} %param.7, bf16[1,512,7168]{2,1,0:T(8,128)(2,1)} %all-gather.7.cloned.1.call-done), kind=kOutput, calls=%fused_computation | convolution fusion | flops 30068965376 | bytes 70258688 | tf_op jit(solution)/shard_map/to,qoi->tqi/dot_general | solution.py:28
  166.8 31.8 %all-reduce = (f32[1,512,2]{1,0,2:T(1,128)S(1)}, f32[1,512,2]{1,0,2:T(1,128)S(1)}) all-reduce(f32[1,512,2]{1,0,2:T(1,128)S(1)} %stack.10, f32[1,512,2]{1,0,2:T(1,128)S(1)} %stack.9), channel_id=1, replica_groups=mesh['grp'=2,'inp'=4,'out'=4] {'inp','out'}, use_global_device_ids=true, to_apply=%region_3.4 | all-reduce | flops 2048 | bytes 16384 | tf_op jit(solution)/shard_map/psum | solution.py:35
  198.7 0.6 fusion.4
  (5 shorter events, 0.1 us)
Async XLA Ops:
  6.5 82.4 %all-gather.5.cloned.1.call-start = ((), (), s32[]{:S(2)}) async-start(), calls=%async_computation | async-start | bytes 9175040 | tf_op jit(solution)/shard_map/all_gather | solution.py:30
  10.6 1.2 copy-start.1
  10.7 117.3 %all-gather.7.cloned.1.call-start = ((), (), s32[]{:S(2)}) async-start(), calls=%async_computation.1 | async-start | bytes 9175040 | tf_op jit(solution)/shard_map/all_gather | solution.py:30
  13.0 18.2 %collective-permute-start = (bf16[128,2048]{1,0:T(8,128)(2,1)}, bf16[128,2048]{1,0:T(8,128)(2,1)}, u32[]{:S(2)}, u32[]{:S(2)}) collective-permute-start(bf16[128,2048]{1,0:T(8,128)(2,1)} %get-tuple-element.9), channel_id=1, source_target_pairs={{0,1},{1,2},{2,3},{3,0},{4,5},{5,6},{6,7},{7,4},{8,9},{9,10},{10,1... | collective-permute-start | bytes 1572872 | tf_op jit(solution)/shard_map/ppermute | solution.py:26
  16.0 26.3 %collective-permute-start.3 = (bf16[128,2048]{1,0:T(8,128)(2,1)}, bf16[128,2048]{1,0:T(8,128)(2,1)}, u32[]{:S(2)}, u32[]{:S(2)}) collective-permute-start(bf16[128,2048]{1,0:T(8,128)(2,1)} %get-tuple-element.10), channel_id=1, source_target_pairs={{0,1},{1,2},{2,3},{3,0},{4,5},{5,6},{6,7},{7,4},{8,9},{9,10},{10,1... | collective-permute-start | bytes 1572872 | tf_op jit(solution)/shard_map/ppermute | solution.py:26
  17.8 13.3 %copy-start.2 = (s32[2,512]{1,0:T(2,128)S(1)}, s32[2,512]{1,0:T(2,128)}, u32[]{:S(2)}) copy-start(s32[2,512]{1,0:T(2,128)} %param.8) | copy-start | bytes 12292
  17.9 24.5 %copy-start.3 = (s32[2,512]{1,0:T(2,128)S(1)}, s32[2,512]{1,0:T(2,128)}, u32[]{:S(2)}) copy-start(s32[2,512]{1,0:T(2,128)} %param.9) | copy-start | bytes 12292
  17.9 1.3 copy-start
  31.1 22.4 %collective-permute-start.1 = (bf16[128,2048]{1,0:T(8,128)(2,1)}, bf16[128,2048]{1,0:T(8,128)(2,1)S(1)}, u32[]{:S(2)}, u32[]{:S(2)}) collective-permute-start(bf16[128,2048]{1,0:T(8,128)(2,1)} %collective-permute-done), channel_id=1, source_target_pairs={{0,1},{1,2},{2,3},{3,0},{4,5},{5,6},{6,7},{7,4},{8,9},{9,10},{10,1... | collective-permute-start | bytes 1572872 | tf_op jit(solution)/shard_map/ppermute | solution.py:26
  42.4 22.4 %collective-permute-start.4 = (bf16[128,2048]{1,0:T(8,128)(2,1)}, bf16[128,2048]{1,0:T(8,128)(2,1)S(1)}, u32[]{:S(2)}, u32[]{:S(2)}) collective-permute-start(bf16[128,2048]{1,0:T(8,128)(2,1)} %collective-permute-done.3), channel_id=1, source_target_pairs={{0,1},{1,2},{2,3},{3,0},{4,5},{5,6},{6,7},{7,4},{8,9},{9,10},{10,1... | collective-permute-start | bytes 1572872 | tf_op jit(solution)/shard_map/ppermute | solution.py:26
  53.5 22.5 %collective-permute-start.2 = (bf16[128,2048]{1,0:T(8,128)(2,1)S(1)}, bf16[128,2048]{1,0:T(8,128)(2,1)S(1)}, u32[]{:S(2)}, u32[]{:S(2)}) collective-permute-start(bf16[128,2048]{1,0:T(8,128)(2,1)S(1)} %collective-permute-done.1), channel_id=1, source_target_pairs={{0,1},{1,2},{2,3},{3,0},{4,5},{5,6},{6,7},{7,4},{8,9},{9,10},{10,1... | collective-permute-start | bytes 1572872 | tf_op jit(solution)/shard_map/ppermute | solution.py:26
  64.7 21.6 %collective-permute-start.5 = (bf16[128,2048]{1,0:T(8,128)(2,1)S(1)}, bf16[128,2048]{1,0:T(8,128)(2,1)S(1)}, u32[]{:S(2)}, u32[]{:S(2)}) collective-permute-start(bf16[128,2048]{1,0:T(8,128)(2,1)S(1)} %collective-permute-done.4), channel_id=1, source_target_pairs={{0,1},{1,2},{2,3},{3,0},{4,5},{5,6},{6,7},{7,4},{8,9},{9,10},{10,1... | collective-permute-start | bytes 1572872 | tf_op jit(solution)/shard_map/ppermute | solution.py:26
Sparse Core Ops, SparseCore 0:
  10.8 55.0 all-gather.4
  67.4 52.2 all-gather.6
